TPU v7x, 32 devices: a whole 2x2x4 slice. The times are simulated.
32 devices in a mesh: groups: 2 (over x), fsdp: 16 (over z, y, core).
Axes of the slice: x: 2, y: 2, z: 4, core: 2. Of those that a mesh axis runs over, the one named last changes fastest.
Arguments:
- obs_feat: bfloat16 [12288, 2048], P(('groups', 'fsdp')), parts along dimension 0, may hold values from -6 to 6
- reward: float32 [512, 24], P(('groups', 'fsdp')), parts along dimension 0, may hold values from -22 to 22
- value_old: float32 [512, 25], P(('groups', 'fsdp')), parts along dimension 0, may hold values from -6 to 6
- done: int32 [512, 24], P(('groups', 'fsdp')), parts along dimension 0, may hold values 0 or 1
- minibatch_perm: int32 [12288], P(('groups', 'fsdp')), parts along dimension 0, may hold values from 0 to 6143, as said below
- old_mean: bfloat16 [12288, 12], P(('groups', 'fsdp')), parts along dimension 0, may hold values from -6 to 6
- noise: bfloat16 [12288, 12], P(('groups', 'fsdp')), parts along dimension 0, may hold values from -6 to 6
- gain_in: float32 [2048], replicated, may hold values from 0.5 to 1.5
- out_weight: bfloat16 [2048, 2048], P('fsdp'), may hold values from -0.125 to 0.125
- head_weight: bfloat16 [2048, 13], replicated, may hold values from -0.125 to 0.125
- log_std: float32 [12], replicated, may hold values from 0.7 to 1.3
Outputs:
- hidden_out: bfloat16 [12288, 2048], P(('groups', 'fsdp')), parts along dimension 0
- grad_weight: float32 [4096, 2048], P(('groups', 'fsdp')), parts along dimension 0
- grad_head: float32 [4096, 13], P('groups'), parts along dimension 0
- grad_std: float32 [24], P('groups'), parts along dimension 0
There are 2 independent parts, one for each index of `groups`. A program takes and returns all parts, laid end to end along the dimension named above; an argument that names none is the same for every part. Nothing has to cross between parts.
Inputs may be any that keep to these rules, and one draw needn't show every extreme that they name: `minibatch_perm`: rows of one index of fsdp go 24 to each index of fsdp; the block of 384 minibatch positions of index j holds at positions j * 384 + s * 24 + c the rows from index s; a permutation of all rows.
All inputs are finite; a program needn't handle non-finite values. No bound on the sum of `done` on one device may be relied on, other than what follows from the above.
Results may differ from a plain program's by a relative error of at most 0.0095.
Values may be sent and summed in bfloat16 or wider, within the bound.
A program may use at most 128 MiB of HBM per device.

v0:
```python
import jax
import jax.numpy as jnp
from jax import lax
from jax.sharding import PartitionSpec as P

GAMMA = 0.99
LAMBDA_GAE = 0.95
CLIP_EPS = 0.2
NORM_EPS = 1e-05


def advantages(reward, value_old, done):
    keep = 1.0 - done.astype(jnp.float32)
    deltas = reward + GAMMA * value_old[:, 1:] * keep - value_old[:, :-1]

    def walk(carry, inputs):
        dstep, kstep = inputs
        carry = dstep + GAMMA * LAMBDA_GAE * kstep * carry
        return (carry, carry)

    start = jnp.zeros((reward.shape[0],), jnp.float32)
    _, stacked = lax.scan(walk, start, (deltas.T, keep.T), reverse=True)
    gae = stacked.T
    return (gae.reshape(-1), (gae + value_old[:, :-1]).reshape(-1))


def compute_rows(
    rows_x, old_mean, noise, adv_b, ret_b, gain_in, out_weight, head_weight, log_std, scale
):
    xf = rows_x.astype(jnp.float32)
    normed = (xf * lax.rsqrt(jnp.mean(xf * xf, -1, keepdims=True) + NORM_EPS) * gain_in).astype(
        jnp.bfloat16
    )
    columns = normed
    hidden = xf + jnp.dot(
        columns,
        lax.all_gather(out_weight, "fsdp", axis=0, tiled=True),
        preferred_element_type=jnp.float32,
    )
    rinv = lax.rsqrt(jnp.mean(hidden * hidden, -1, keepdims=True) + NORM_EPS)
    hnorm = hidden * rinv
    hnorm_b = hnorm.astype(jnp.bfloat16)
    heads = jnp.dot(hnorm_b, head_weight, preferred_element_type=jnp.float32)
    nact = log_std.shape[0]
    mean_act = heads[:, :nact]
    value = heads[:, nact]
    std_dev = jnp.exp(log_std)
    offset = old_mean.astype(jnp.float32) - mean_act
    sample = noise.astype(jnp.float32)
    logr = jnp.sum(-sample * offset / std_dev - offset * offset / (2.0 * std_dev * std_dev), -1)
    ratio = jnp.exp(logr)
    advant = adv_b.astype(jnp.float32)
    clipped = jnp.clip(ratio, 1.0 - CLIP_EPS, 1.0 + CLIP_EPS)
    active = ratio * advant <= clipped * advant
    gratio = jnp.where(active, -scale * advant, 0.0)
    glogr = gratio * ratio
    gmean = glogr[:, None] * (sample / std_dev + offset / (std_dev * std_dev))
    gvalue = scale * (value - ret_b.astype(jnp.float32))
    std_local = jnp.sum(
        glogr[:, None] * (sample * offset / std_dev + offset * offset / (std_dev * std_dev)), 0
    )
    ghead = jnp.concatenate([gmean, gvalue[:, None]], 1)
    head_local = jnp.dot(hnorm_b.astype(jnp.float32).T, ghead, precision=lax.Precision.HIGHEST)
    ghn = jnp.dot(ghead, head_weight.astype(jnp.float32).T, precision=lax.Precision.HIGHEST)
    ghid = rinv * (ghn - hnorm * jnp.mean(ghn * hnorm, -1, keepdims=True))
    ghid_b = ghid.astype(jnp.bfloat16)
    columns = normed
    grad_weight = lax.psum_scatter(
        lax.dot_general(
            columns, ghid_b, (((0,), (0,)), ((), ())), preferred_element_type=jnp.float32
        ),
        "fsdp",
        scatter_dimension=0,
        tiled=True,
    )
    grad_head, grad_std = lax.psum((head_local, std_local), "fsdp")
    return (hidden.astype(jnp.bfloat16), grad_weight, grad_head, grad_std)


def local(
    obs_feat,
    reward,
    value_old,
    done,
    minibatch_perm,
    old_mean,
    noise,
    gain_in,
    out_weight,
    head_weight,
    log_std,
):
    gae, returns = advantages(reward, value_old, done)
    local_rows = obs_feat.shape[0]
    devices = lax.axis_size("fsdp")
    total_rows = local_rows * devices
    sums, squares = lax.psum((jnp.sum(gae), jnp.sum(gae * gae)), "fsdp")
    mean_adv = sums / total_rows
    var_adv = squares / total_rows - mean_adv * mean_adv
    adv_b = ((gae - mean_adv) * lax.rsqrt(var_adv + NORM_EPS)).astype(jnp.bfloat16)
    ret_b = returns.astype(jnp.bfloat16)
    scale = 1.0 / jnp.sqrt(jnp.float32(total_rows))
    per_peer = local_rows // devices
    send_slot = minibatch_perm // local_rows * per_peer + minibatch_perm % per_peer
    hidden_local, grad_weight, grad_head, grad_std = compute_rows(
        obs_feat, old_mean, noise, adv_b, ret_b, gain_in, out_weight, head_weight, log_std, scale
    )
    send_hidden = jnp.zeros_like(hidden_local).at[send_slot].set(hidden_local)
    hidden_out = lax.all_to_all(send_hidden, "fsdp", split_axis=0, concat_axis=0, tiled=True)
    return (hidden_out, grad_weight, grad_head, grad_std)


def solution(mesh):
    return jax.shard_map(
        local,
        mesh=mesh,
        in_specs=(
            P(("groups", "fsdp"), None),
            P(("groups", "fsdp"), None),
            P(("groups", "fsdp"), None),
            P(("groups", "fsdp"), None),
            P(("groups", "fsdp")),
            P(("groups", "fsdp"), None),
            P(("groups", "fsdp"), None),
            P(),
            P("fsdp", None),
            P(),
            P(),
        ),
        out_specs=(
            P(("groups", "fsdp"), None),
            P(("groups", "fsdp"), None),
            P("groups", None),
            P("groups"),
        ),
        check_vma=False,
    )
```

profile of v0, /device:TPU:0, one launch (start us, length us, event | category | flops | bytes accessed | tf_op | source)
XLA Modules:
  0.0 389.4 jit_solution(8685224248298809231)
XLA Ops:
  7.2 0.0 copy-start
  7.2 0.0 all-gather.2.cloned.1.call-start
  7.2 0.7 all-gather.2.cloned.1.call-update
  7.9 0.0 all-reduce.3.cloned.1.call-start
  8.0 0.9 fusion.31
  8.8 0.1 copy.26
  8.9 0.1 copy.27
  9.0 1.8 while.17
  10.8 0.1 copy.28
  10.8 0.6 fusion.29
  11.5 0.6 reduce_sum.66
  12.1 36.7 %all-reduce = (f32[]{:T(128)}, f32[]{:T(128)}) all-reduce(f32[]{:T(128)} %fusion.29, f32[]{:T(128)} %reduce_sum.66), channel_id=1, replica_groups=mesh['groups'=2,'fsdp'=16] {'fsdp'}, use_global_device_ids=true, to_apply=%region_9.10 | all-reduce | flops 2 | bytes 16 | tf_op jit(solution)/shard_map/psum | solution.py:97
  51.4 0.7 fusion.33
  52.1 0.1 reshape.79
  52.2 0.1 reshape.80
  52.3 1.8 fusion.2
  54.1 0.7 fusion.39
  54.8 32.7 %all-gather.2.cloned.1.call-done = bf16[2048,2048]{1,0:T(8,128)(2,1)} async-done(((bf16[128,2048]{1,0:T(8,128)(2,1)}), bf16[2048,2048]{1,0:T(8,128)(2,1)}) %all-gather.2.cloned.1.call-update) | async-done | bytes 8388624 | tf_op jit(solution)/shard_map/all_gather | solution.py:37
  87.5 7.9 %multiply_reduce_fusion.1 = (f32[384]{0:T(512)S(1)}, f32[384,2048]{1,0:T(8,128)S(1)}) fusion(bf16[2048,2048]{1,0:T(8,128)(2,1)} %all-gather.2.cloned.1.call-done, bf16[384,2048]{1,0:T(8,128)(2,1)} %param.13, f32[2048]{0:T(1024)} %param.20, f32[384]{0:T(512)S(1)} %add_rsqrt_fusion.1), kind=kOutput, calls=%fused_computation.12 | convolution fusion | flops 3227516416 | bytes 13118464 | tf_op jit(solution)/shard_map/dot_general | solution.py:35
  95.3 0.0 copy-start.2
  95.3 0.0 copy-start.3
  95.4 0.2 multiply_convert_fusion.1
  95.6 0.0 copy-done
  95.6 0.5 fusion.40
  96.1 0.0 copy-done.2
  96.1 0.0 copy-done.3
  96.2 0.1 fusion.23
  96.3 0.2 fusion.24
  96.5 0.0 copy-start.4
  96.5 3.4 multiply_reduce_fusion
  99.8 1.4 fusion.25
  101.2 0.0 all-reduce.3.cloned.1.call-update
  101.3 0.2 reduce-scatter.2.cloned.1.call-start
  101.5 0.0 copy-done.4
  101.5 12.9 %fusion.5 = f32[2048,2048]{1,0:T(8,128)} fusion(f32[384,2048]{1,0:T(8,128)} %get-tuple-element.155, f32[384,2048]{1,0:T(8,128)S(1)} %get-tuple-element.153, f32[384]{0:T(512)S(1)} %broadcast_multiply_fusion, f32[384]{0:T(512)S(1)} %add_rsqrt_fusion, bf16[384,2048]{1,0:T(8,128)(2,1)} %param.13, f32[2048]{0:T(1024)S(1)} %copy-done.4, f32[384]{0:T(512)S(1)} %add_rsqrt_fusion.1), kind=kOutput, calls=%fused_computation.14 | convolution fusion | flops 3228303360 | bytes 24654336 | tf_op jit(solution)/shard_map/dot_general | solution.py:69
  114.4 0.0 copy-start.5
  114.4 0.0 reduce-scatter.2.cloned.1.call-update
  114.4 0.7 copy-done.5
  115.1 4.1 %scatter_custom_fusion = bf16[384,2048]{1,0:T(8,128)(2,1)} fusion(s32[384]{0:T(512)S(1)} %compare_select_fusion, f32[384,2048]{1,0:T(8,128)S(1)} %get-tuple-element.153, bf16[]{:T(256)} %constant.88.clone.1), kind=kCustom, calls=%fused_computation.17 | custom fusion | flops 786432 | bytes 4718594 | tf_op jit(solution)/shard_map/scatter | solution.py:108
  119.2 3.7 all-to-all-start
  122.9 54.6 %psum.31 = f32[12]{0:T(128)} all-reduce(f32[12]{0:T(128)S(1)} %get-tuple-element.143), channel_id=1, replica_groups=mesh['groups'=2,'fsdp'=16] {'fsdp'}, use_global_device_ids=true, to_apply=%region_14.15 | all-reduce | flops 12 | bytes 96 | tf_op jit(solution)/shard_map/psum | solution.py:76
  177.5 0.0 all-to-all-done
  177.5 20.0 %all-reduce.3.cloned.1.call-done = f32[2048,13]{0,1:T(8,128)} async-done(((f32[2048,13]{0,1:T(8,128)}), f32[2048,13]{0,1:T(8,128)}) %all-reduce.3.cloned.1.call-update) | async-done | bytes 106512 | tf_op jit(solution)/shard_map/psum | solution.py:76
  197.5 0.0 copy-start.1
  197.5 183.6 %reduce-scatter.2.cloned.1.call-done = f32[128,2048]{1,0:T(8,128)} async-done(((f32[2048,2048]{1,0:T(8,128)}), f32[128,2048]{1,0:T(8,128)}) %reduce-scatter.2.cloned.1.call-update) | async-done | bytes 1048592 | tf_op jit(solution)/shard_map/reduce_scatter | solution.py:68
  381.1 1.1 copy.41
  382.2 0.0 copy-done.1
  382.2 0.7 copy.42
  (56 shorter events, 1.5 us)
Async XLA Ops:
  7.2 88.4 %copy-start = (bf16[2048,13]{0,1:T(8,128)(2,1)S(1)}, bf16[2048,13]{0,1:T(8,128)(2,1)}, u32[]{:S(2)}) copy-start(bf16[2048,13]{0,1:T(8,128)(2,1)} %param.22) | copy-start | bytes 159748
  7.2 80.3 %all-gather.2.cloned.1.call-start = ((), (), s32[]{:S(2)}) async-start(), calls=%async_computation.2 | async-start | bytes 8912896 | tf_op jit(solution)/shard_map/all_gather | solution.py:37
  7.9 189.6 %all-reduce.3.cloned.1.call-start = ((), (), s32[]{:S(2)}) async-start(), calls=%async_computation.4 | async-start | bytes 262144 | tf_op jit(solution)/shard_map/psum | solution.py:76
  95.3 0.8 copy-start.2
  95.3 0.8 copy-start.3
  96.5 5.0 %copy-start.4 = (f32[2048]{0:T(1024)S(1)}, f32[2048]{0:T(1024)}, u32[]{:S(2)}) copy-start(f32[2048]{0:T(1024)} %param.20) | copy-start | bytes 24580
  101.3 279.8 %reduce-scatter.2.cloned.1.call-start = ((), (), s32[]{:S(2)}) async-start(), calls=%async_computation.3 | async-start | bytes 17825792 | tf_op jit(solution)/shard_map/reduce_scatter | solution.py:68
  114.4 0.7 copy-start.5
  119.2 58.3 %all-to-all-start = ((bf16[16,24,2048]{2,1,0:T(8,128)(2,1)}), bf16[16,24,2048]{2,1,0:T(8,128)(2,1)S(1)}, u32[]{:S(2)}, u32[]{:S(2)}) async-start(bf16[16,24,2048]{2,1,0:T(8,128)(2,1)} %bitcast.39), calls=%async_computation | async-start | bytes 3145728 | tf_op jit(solution)/shard_map/all_to_all | solution.py:109
  197.5 184.8 %copy-start.1 = (f32[2048,13]{0,1:T(8,128)S(1)}, f32[2048,13]{0,1:T(8,128)}, u32[]{:S(2)}) copy-start(f32[2048,13]{0,1:T(8,128)} %all-reduce.3.cloned.1.call-done) | copy-start | bytes 319492
Sparse Core Ops, SparseCore 0:
  10.2 77.2 all-gather.1
  101.4 96.0 all-reduce.2
  202.2 178.8 reduce-scatter.1
where the time goes:
time: 390 us; the launch traced here: 389 us
  waiting for transfers between devices  237 us (61%)
  blocking collectives  91.3 us (23%)
  matrix products  26 us (7%)
  between operations  16.5 us (4%)
  other arithmetic  10.4 us (3%)
  starting transfers between devices  4.01 us (1%)
    reduce_scatter x1, waiting for transfers between devices, compute_rows(): lax.psum_scatter(lax.dot_general(columns, ghid_b, (((0,), (0,)), ((), ())...  184 us
    psum x1, blocking collectives, compute_rows(): grad_head, grad_std = lax.psum((head_local, std_local), 'fsdp')  54.6 us
    psum x1, blocking collectives, local(): sums, squares = lax.psum((jnp.sum(gae), jnp.sum(gae * gae)), 'fsdp')  36.7 us
    all_gather x1, waiting for transfers between devices, compute_rows(): lax.all_gather(out_weight, 'fsdp', axis=0, tiled=True)  32.7 us
    psum x1, waiting for transfers between devices, compute_rows(): grad_head, grad_std = lax.psum((head_local, std_local), 'fsdp')  20 us
    dot_general x1, matrix products, compute_rows(): lax.dot_general(columns, ghid_b, (((0,), (0,)), ((), ())), preferred_elem...  12.9 us
    dot_general x1, matrix products, compute_rows(): jnp.dot(columns, lax.all_gather(out_weight, 'fsdp', axis=0, tiled=True),...  7.85 us
  transfers between devices with their start and end apart: 4, of which 3 were waited for; matrix products, arithmetic and copies ran while one was open for 6% of the time, Pallas kernels for 0%

commit v1 on v0

--- a/solution.py
+++ b/solution.py
@@ -27,15 +27,29 @@
 def compute_rows(
     rows_x, old_mean, noise, adv_b, ret_b, gain_in, out_weight, head_weight, log_std, scale
 ):
+
+    def raise_the_islands(array_here, axis_tag):
+        degree = lax.axis_size(axis_tag)
+        line_up = tuple(((s, (s + 1) % degree) for s in range(degree)))
+        piece_out, piece_now = ([array_here], [array_here])
+        pool = tuple(((s, (s - 1) % degree) for s in range(degree)))
+        for _ in range(degree // 2):
+            piece_out.append(lax.ppermute(piece_out[-1], axis_tag, line_up))
+        for _ in [*range((degree - 1) // 2)]:
+            piece_now.append(lax.ppermute(piece_now[-1], axis_tag, pool))
+        return jnp.roll(
+            jnp.concatenate([*piece_out[::-1], *piece_now[1:]], axis=0),
+            (lax.axis_index(axis_tag) - degree // 2) * array_here.shape[0],
+            axis=0,
+        )
+
     xf = rows_x.astype(jnp.float32)
     normed = (xf * lax.rsqrt(jnp.mean(xf * xf, -1, keepdims=True) + NORM_EPS) * gain_in).astype(
         jnp.bfloat16
     )
     columns = normed
     hidden = xf + jnp.dot(
-        columns,
-        lax.all_gather(out_weight, "fsdp", axis=0, tiled=True),
-        preferred_element_type=jnp.float32,
+        columns, raise_the_islands(out_weight, axis_tag="fsdp"), preferred_element_type=jnp.float32
     )
     rinv = lax.rsqrt(jnp.mean(hidden * hidden, -1, keepdims=True) + NORM_EPS)
     hnorm = hidden * rinv

time: 390 us -> 463 us (1.19)
  starting transfers between devices: 4.01 us -> 45.6 us
  local copies, waits for them, and re-layouts: 3.81 us -> 24 us
  waiting for transfers between devices: 237 us -> 256 us
    ppermute x0 -> x15, waiting for transfers between devices: none -> 47.4 us  [the longest x8 43.6 us: raise_the_islands(): piece_out.append(lax.ppermute(piece_out[-1], axis_tag, line_up))]
    ppermute x0 -> x15, starting transfers between devices: none -> 40.1 us  [the longest x8 22.7 us: raise_the_islands(): piece_out.append(lax.ppermute(piece_out[-1], axis_tag, line_up))]
    all_gather x1 -> x0, waiting for transfers between devices: 32.7 us -> none  [compute_rows(): lax.all_gather(out_weight, 'fsdp', axis=0, tiled=True)]
    unnamed x16 -> x53, local copies, waits for them, and re-layouts: 2.63 us -> 22.8 us
  transfers between devices with their start and end apart: 4 -> 18, of which waited for: 3 -> 10; matrix products, arithmetic and copies ran while one was open for 6% -> 8% of each run, Pallas kernels for 0% -> 0%
where the time goes in v1:
time: 463 us; the launch traced here: 462 us
  waiting for transfers between devices  256 us (55%)
  blocking collectives  87.3 us (19%)
  starting transfers between devices  45.6 us (10%)
  local copies, waits for them, and re-layouts  24 us (5%)
  matrix products  21.8 us (5%)
  between operations  17.1 us (4%)
  other arithmetic  10.5 us (2%)
    reduce_scatter x1, waiting for transfers between devices, compute_rows(): lax.psum_scatter(lax.dot_general(columns, ghid_b, (((0,), (0,)), ((), ())...  184 us
    psum x1, blocking collectives, compute_rows(): grad_head, grad_std = lax.psum((head_local, std_local), 'fsdp')  54.7 us
    ppermute x8, waiting for transfers between devices, raise_the_islands(): piece_out.append(lax.ppermute(piece_out[-1], axis_tag, line_up))  43.6 us
    psum x1, blocking collectives, local(): sums, squares = lax.psum((jnp.sum(gae), jnp.sum(gae * gae)), 'fsdp')  32.6 us
    psum x1, waiting for transfers between devices, compute_rows(): grad_head, grad_std = lax.psum((head_local, std_local), 'fsdp')  24.4 us
    unnamed x53, local copies, waits for them, and re-layouts  22.8 us
    ppermute x8, starting transfers between devices, raise_the_islands(): piece_out.append(lax.ppermute(piece_out[-1], axis_tag, line_up))  22.7 us
    ppermute x7, starting transfers between devices, raise_the_islands(): piece_now.append(lax.ppermute(piece_now[-1], axis_tag, pool))  17.4 us
  transfers between devices with their start and end apart: 18, of which 10 were waited for; matrix products, arithmetic and copies ran while one was open for 8% of the time, Pallas kernels for 0%

profile of v1, /device:TPU:0, one launch (start us, length us, event | category | flops | bytes accessed | tf_op | source)
XLA Modules:
  0.0 462.1 jit_solution(7968159435080892518)
XLA Ops:
  7.8 12.1 %collective-permute-done = bf16[128,2048]{1,0:T(8,128)(2,1)S(1)} collective-permute-done((bf16[128,2048]{1,0:T(8,128)(2,1)}, bf16[128,2048]{1,0:T(8,128)(2,1)S(1)}, u32[]{:S(2)}, u32[]{:S(2)}) %collective-permute-start) | collective-permute-done | bytes 524320 | tf_op jit(solution)/shard_map/ppermute | solution.py:37
  19.8 4.4 collective-permute-start.8
  24.3 7.0 %collective-permute-done.1 = bf16[128,2048]{1,0:T(8,128)(2,1)S(1)} collective-permute-done((bf16[128,2048]{1,0:T(8,128)(2,1)S(1)}, bf16[128,2048]{1,0:T(8,128)(2,1)S(1)}, u32[]{:S(2)}, u32[]{:S(2)}) %collective-permute-start.1) | collective-permute-done | bytes 524320 | tf_op jit(solution)/shard_map/ppermute | solution.py:37
  31.3 4.6 collective-permute-start.9
  35.9 6.8 %collective-permute-done.2 = bf16[128,2048]{1,0:T(8,128)(2,1)S(1)} collective-permute-done((bf16[128,2048]{1,0:T(8,128)(2,1)S(1)}, bf16[128,2048]{1,0:T(8,128)(2,1)S(1)}, u32[]{:S(2)}, u32[]{:S(2)}) %collective-permute-start.2) | collective-permute-done | bytes 524320 | tf_op jit(solution)/shard_map/ppermute | solution.py:37
  42.7 1.8 collective-permute-start.3
  44.4 2.9 collective-permute-start.10
  47.3 6.8 %collective-permute-done.3 = bf16[128,2048]{1,0:T(8,128)(2,1)S(1)} collective-permute-done((bf16[128,2048]{1,0:T(8,128)(2,1)S(1)}, bf16[128,2048]{1,0:T(8,128)(2,1)S(1)}, u32[]{:S(2)}, u32[]{:S(2)}) %collective-permute-start.3) | collective-permute-done | bytes 524320 | tf_op jit(solution)/shard_map/ppermute | solution.py:37
  54.1 3.8 collective-permute-start.4
  58.7 6.9 %collective-permute-done.4 = bf16[128,2048]{1,0:T(8,128)(2,1)} collective-permute-done((bf16[128,2048]{1,0:T(8,128)(2,1)S(1)}, bf16[128,2048]{1,0:T(8,128)(2,1)}, u32[]{:S(2)}, u32[]{:S(2)}) %collective-permute-start.4) | collective-permute-done | bytes 524320 | tf_op jit(solution)/shard_map/ppermute | solution.py:37
  65.6 6.5 %collective-permute-start.5 = (bf16[128,2048]{1,0:T(8,128)(2,1)}, bf16[128,2048]{1,0:T(8,128)(2,1)}, u32[]{:S(2)}, u32[]{:S(2)}) collective-permute-start(bf16[128,2048]{1,0:T(8,128)(2,1)} %collective-permute-done.4), channel_id=1, source_target_pairs={{0,1},{1,2},{2,3},{3,4},{4,5},{5,6},{6,7},{7,8},{8,9},{9,10},{10,1... | collective-permute-start | bytes 1572872 | tf_op jit(solution)/shard_map/ppermute | solution.py:37
  72.1 0.8 fusion.35
  73.1 4.1 collective-permute-done.5
  77.2 9.6 %collective-permute-start.6 = (bf16[128,2048]{1,0:T(8,128)(2,1)}, bf16[128,2048]{1,0:T(8,128)(2,1)}, u32[]{:S(2)}, u32[]{:S(2)}) collective-permute-start(bf16[128,2048]{1,0:T(8,128)(2,1)} %collective-permute-done.5), channel_id=1, source_target_pairs={{0,1},{1,2},{2,3},{3,4},{4,5},{5,6},{6,7},{7,8},{8,9},{9,10},{10,1... | collective-permute-start | bytes 1572872 | tf_op jit(solution)/shard_map/ppermute | solution.py:37
  86.7 1.8 while.17
  89.8 32.6 %all-reduce = (f32[]{:T(128)}, f32[]{:T(128)}) all-reduce(f32[]{:T(128)} %fusion.33, f32[]{:T(128)} %reduce_sum.66), channel_id=1, replica_groups=mesh['groups'=2,'fsdp'=16] {'fsdp'}, use_global_device_ids=true, to_apply=%region_9.10 | all-reduce | flops 2 | bytes 16 | tf_op jit(solution)/shard_map/psum | solution.py:111
  126.3 1.8 fusion.4
  129.0 3.8 collective-permute-done.13
  132.8 4.6 collective-permute-start.14
  137.5 1.1 constant_dynamic-update-slice_fusion.31
  138.6 1.1 constant_dynamic-update-slice_fusion.30
  139.7 1.1 constant_dynamic-update-slice_fusion.29
  140.8 1.1 constant_dynamic-update-slice_fusion.28
  141.9 1.1 constant_dynamic-update-slice_fusion.27
  143.1 1.1 constant_dynamic-update-slice_fusion.23
  144.2 1.1 constant_dynamic-update-slice_fusion.20
  145.3 1.1 constant_dynamic-update-slice_fusion.19
  146.4 1.1 constant_dynamic-update-slice_fusion.18
  147.5 1.1 constant_dynamic-update-slice_fusion.17
  148.6 1.1 constant_dynamic-update-slice_fusion.15
  149.7 1.1 constant_dynamic-update-slice_fusion.14
  150.8 1.1 constant_dynamic-update-slice_fusion.13
  151.9 1.1 constant_dynamic-update-slice_fusion.12
  153.3 1.1 constant_dynamic-update-slice_fusion.4
  154.4 1.1 constant_dynamic-update-slice_fusion.3
  155.4 1.1 constant_dynamic-update-slice_fusion.2
  156.5 1.1 constant_dynamic-update-slice_fusion.1
  157.7 3.6 multiply_reduce_fusion.1
  162.5 1.4 fusion.29
  163.8 3.4 multiply_reduce_fusion
  167.5 12.9 %fusion.9 = f32[2048,2048]{1,0:T(8,128)} fusion(f32[384,2048]{1,0:T(8,128)} %get-tuple-element.155, f32[384,2048]{1,0:T(8,128)S(1)} %get-tuple-element.153, f32[384]{0:T(512)S(1)} %broadcast_multiply_fusion, f32[384]{0:T(512)S(1)} %add_rsqrt_fusion, bf16[384,2048]{1,0:T(8,128)(2,1)} %param.13, f32[2048]{0:T(1024)S(1)} %copy-done.7, f32[384]{0:T(512)S(1)} %add_rsqrt_fusion.1), kind=kOutput, calls=%fused_computation.16 | convolution fusion | flops 3228303360 | bytes 24654336 | tf_op jit(solution)/shard_map/dot_general | solution.py:83
  180.4 4.1 scatter_custom_fusion
  184.5 5.3 %all-to-all-start = ((bf16[16,24,2048]{2,1,0:T(8,128)(2,1)}), bf16[16,24,2048]{2,1,0:T(8,128)(2,1)S(1)}, u32[]{:S(2)}, u32[]{:S(2)}) async-start(bf16[16,24,2048]{2,1,0:T(8,128)(2,1)} %bitcast.38), calls=%async_computation | async-start | bytes 3145728 | tf_op jit(solution)/shard_map/all_to_all | solution.py:123
  189.8 54.7 %psum.31 = f32[12]{0:T(128)} all-reduce(f32[12]{0:T(128)S(1)} %get-tuple-element.143), channel_id=1, replica_groups=mesh['groups'=2,'fsdp'=16] {'fsdp'}, use_global_device_ids=true, to_apply=%region_14.15 | all-reduce | flops 12 | bytes 96 | tf_op jit(solution)/shard_map/psum | solution.py:90
  244.5 24.4 %all-reduce.3.cloned.1.call-done = f32[2048,13]{0,1:T(8,128)} async-done(((f32[2048,13]{0,1:T(8,128)}), f32[2048,13]{0,1:T(8,128)}) %all-reduce.3.cloned.1.call-update) | async-done | bytes 106512 | tf_op jit(solution)/shard_map/psum | solution.py:90
  269.0 183.6 %reduce-scatter.2.cloned.1.call-done = f32[128,2048]{1,0:T(8,128)} async-done(((f32[2048,2048]{1,0:T(8,128)}), f32[128,2048]{1,0:T(8,128)}) %reduce-scatter.2.cloned.1.call-update) | async-done | bytes 1048592 | tf_op jit(solution)/shard_map/reduce_scatter | solution.py:82
  452.6 1.1 copy.72
  453.7 1.6 copy.73
  (121 shorter events, 8.5 us)
Async XLA Ops:
  7.2 154.4 %copy-start = (bf16[2048,13]{0,1:T(8,128)(2,1)S(1)}, bf16[2048,13]{0,1:T(8,128)(2,1)}, u32[]{:S(2)}) copy-start(bf16[2048,13]{0,1:T(8,128)(2,1)} %param.22) | copy-start | bytes 159748
  7.2 146.0 %copy-start.2 = (bf16[128,2048]{1,0:T(8,128)(2,1)S(1)}, bf16[128,2048]{1,0:T(8,128)(2,1)}, u32[]{:S(2)}) copy-start(bf16[128,2048]{1,0:T(8,128)(2,1)} %param.21) | copy-start | bytes 1572868
  7.2 261.8 %all-reduce.3.cloned.1.call-start = ((), (), s32[]{:S(2)}) async-start(), calls=%async_computation.3 | async-start | bytes 262144 | tf_op jit(solution)/shard_map/psum | solution.py:90
  7.2 12.6 %collective-permute-start = (bf16[128,2048]{1,0:T(8,128)(2,1)}, bf16[128,2048]{1,0:T(8,128)(2,1)S(1)}, u32[]{:S(2)}, u32[]{:S(2)}) collective-permute-start(bf16[128,2048]{1,0:T(8,128)(2,1)} %param.21), channel_id=1, source_target_pairs={{0,1},{1,2},{2,3},{3,4},{4,5},{5,6},{6,7},{7,8},{8,9},{9,10},{10,1... | collective-permute-start | bytes 1572872 | tf_op jit(solution)/shard_map/ppermute | solution.py:37
  19.8 11.4 %collective-permute-start.1 = (bf16[128,2048]{1,0:T(8,128)(2,1)S(1)}, bf16[128,2048]{1,0:T(8,128)(2,1)S(1)}, u32[]{:S(2)}, u32[]{:S(2)}) collective-permute-start(bf16[128,2048]{1,0:T(8,128)(2,1)S(1)} %collective-permute-done), channel_id=1, source_target_pairs={{0,1},{1,2},{2,3},{3,4},{4,5},{5,6},{6,7},{7,8},{8,9},{9,10},{10,1... | collective-permute-start | bytes 1572872 | tf_op jit(solution)/shard_map/ppermute | solution.py:37
  19.8 11.5 %collective-permute-start.8 = (bf16[128,2048]{1,0:T(8,128)(2,1)}, bf16[128,2048]{1,0:T(8,128)(2,1)S(1)}, u32[]{:S(2)}, u32[]{:S(2)}) collective-permute-start(bf16[128,2048]{1,0:T(8,128)(2,1)} %param.21), channel_id=1, source_target_pairs={{0,15},{1,0},{2,1},{3,2},{4,3},{5,4},{6,5},{7,6},{8,7},{9,8},{10,9... | collective-permute-start | bytes 1572872 | tf_op jit(solution)/shard_map/ppermute | solution.py:39
  31.2 11.4 %collective-permute-start.2 = (bf16[128,2048]{1,0:T(8,128)(2,1)S(1)}, bf16[128,2048]{1,0:T(8,128)(2,1)S(1)}, u32[]{:S(2)}, u32[]{:S(2)}) collective-permute-start(bf16[128,2048]{1,0:T(8,128)(2,1)S(1)} %collective-permute-done.1), channel_id=1, source_target_pairs={{0,1},{1,2},{2,3},{3,4},{4,5},{5,6},{6,7},{7,8},{8,9},{9,10},{10,1... | collective-permute-start | bytes 1572872 | tf_op jit(solution)/shard_map/ppermute | solution.py:37
  31.3 13.1 %collective-permute-start.9 = (bf16[128,2048]{1,0:T(8,128)(2,1)S(1)}, bf16[128,2048]{1,0:T(8,128)(2,1)S(1)}, u32[]{:S(2)}, u32[]{:S(2)}) collective-permute-start(bf16[128,2048]{1,0:T(8,128)(2,1)S(1)} %collective-permute-done.8), channel_id=1, source_target_pairs={{0,15},{1,0},{2,1},{3,2},{4,3},{5,4},{6,5},{7,6},{8,7},{9,8},{10,9... | collective-permute-start | bytes 1572872 | tf_op jit(solution)/shard_map/ppermute | solution.py:39
  42.7 11.4 %collective-permute-start.3 = (bf16[128,2048]{1,0:T(8,128)(2,1)S(1)}, bf16[128,2048]{1,0:T(8,128)(2,1)S(1)}, u32[]{:S(2)}, u32[]{:S(2)}) collective-permute-start(bf16[128,2048]{1,0:T(8,128)(2,1)S(1)} %collective-permute-done.2), channel_id=1, source_target_pairs={{0,1},{1,2},{2,3},{3,4},{4,5},{5,6},{6,7},{7,8},{8,9},{9,10},{10,1... | collective-permute-start | bytes 1572872 | tf_op jit(solution)/shard_map/ppermute | solution.py:37
  44.4 13.5 %collective-permute-start.10 = (bf16[128,2048]{1,0:T(8,128)(2,1)S(1)}, bf16[128,2048]{1,0:T(8,128)(2,1)}, u32[]{:S(2)}, u32[]{:S(2)}) collective-permute-start(bf16[128,2048]{1,0:T(8,128)(2,1)S(1)} %collective-permute-done.9), channel_id=1, source_target_pairs={{0,15},{1,0},{2,1},{3,2},{4,3},{5,4},{6,5},{7,6},{8,7},{9,8},{10,9... | collective-permute-start | bytes 1572872 | tf_op jit(solution)/shard_map/ppermute | solution.py:39
  54.1 3.8 copy-start.3
  54.1 11.5 %collective-permute-start.4 = (bf16[128,2048]{1,0:T(8,128)(2,1)S(1)}, bf16[128,2048]{1,0:T(8,128)(2,1)}, u32[]{:S(2)}, u32[]{:S(2)}) collective-permute-start(bf16[128,2048]{1,0:T(8,128)(2,1)S(1)} %collective-permute-done.3), channel_id=1, source_target_pairs={{0,1},{1,2},{2,3},{3,4},{4,5},{5,6},{6,7},{7,8},{8,9},{9,10},{10,1... | collective-permute-start | bytes 1572872 | tf_op jit(solution)/shard_map/ppermute | solution.py:37
  57.9 15.2 %collective-permute-start.11 = (bf16[128,2048]{1,0:T(8,128)(2,1)}, bf16[128,2048]{1,0:T(8,128)(2,1)}, u32[]{:S(2)}, u32[]{:S(2)}) collective-permute-start(bf16[128,2048]{1,0:T(8,128)(2,1)} %collective-permute-done.10), channel_id=1, source_target_pairs={{0,15},{1,0},{2,1},{3,2},{4,3},{5,4},{6,5},{7,6},{8,7},{9,8},{10,9... | collective-permute-start | bytes 1572872 | tf_op jit(solution)/shard_map/ppermute | solution.py:39
  65.6 11.6 %collective-permute-start.5 = (bf16[128,2048]{1,0:T(8,128)(2,1)}, bf16[128,2048]{1,0:T(8,128)(2,1)}, u32[]{:S(2)}, u32[]{:S(2)}) collective-permute-start(bf16[128,2048]{1,0:T(8,128)(2,1)} %collective-permute-done.4), channel_id=1, source_target_pairs={{0,1},{1,2},{2,3},{3,4},{4,5},{5,6},{6,7},{7,8},{8,9},{9,10},{10,1... | collective-permute-start | bytes 1572872 | tf_op jit(solution)/shard_map/ppermute | solution.py:37
  73.1 52.6 %collective-permute-start.12 = (bf16[128,2048]{1,0:T(8,128)(2,1)}, bf16[128,2048]{1,0:T(8,128)(2,1)}, u32[]{:S(2)}, u32[]{:S(2)}) collective-permute-start(bf16[128,2048]{1,0:T(8,128)(2,1)} %collective-permute-done.11), channel_id=1, source_target_pairs={{0,15},{1,0},{2,1},{3,2},{4,3},{5,4},{6,5},{7,6},{8,7},{9,8},{10,9... | collective-permute-start | bytes 1572872 | tf_op jit(solution)/shard_map/ppermute | solution.py:39
  77.2 48.6 %collective-permute-start.6 = (bf16[128,2048]{1,0:T(8,128)(2,1)}, bf16[128,2048]{1,0:T(8,128)(2,1)}, u32[]{:S(2)}, u32[]{:S(2)}) collective-permute-start(bf16[128,2048]{1,0:T(8,128)(2,1)} %collective-permute-done.5), channel_id=1, source_target_pairs={{0,1},{1,2},{2,3},{3,4},{4,5},{5,6},{6,7},{7,8},{8,9},{9,10},{10,1... | collective-permute-start | bytes 1572872 | tf_op jit(solution)/shard_map/ppermute | solution.py:37
  125.7 7.0 %collective-permute-start.13 = (bf16[128,2048]{1,0:T(8,128)(2,1)}, bf16[128,2048]{1,0:T(8,128)(2,1)}, u32[]{:S(2)}, u32[]{:S(2)}) collective-permute-start(bf16[128,2048]{1,0:T(8,128)(2,1)} %collective-permute-done.12), channel_id=1, source_target_pairs={{0,15},{1,0},{2,1},{3,2},{4,3},{5,4},{6,5},{7,6},{8,7},{9,8},{10,9... | collective-permute-start | bytes 1572872 | tf_op jit(solution)/shard_map/ppermute | solution.py:39
  125.8 11.8 %collective-permute-start.7 = (bf16[128,2048]{1,0:T(8,128)(2,1)}, bf16[128,2048]{1,0:T(8,128)(2,1)}, u32[]{:S(2)}, u32[]{:S(2)}) collective-permute-start(bf16[128,2048]{1,0:T(8,128)(2,1)} %collective-permute-done.6), channel_id=1, source_target_pairs={{0,1},{1,2},{2,3},{3,4},{4,5},{5,6},{6,7},{7,8},{8,9},{9,10},{10,1... | collective-permute-start | bytes 1572872 | tf_op jit(solution)/shard_map/ppermute | solution.py:37
  128.3 24.7 %copy-start.4 = (bf16[128,2048]{1,0:T(8,128)(2,1)S(1)}, bf16[128,2048]{1,0:T(8,128)(2,1)}, u32[]{:S(2)}) copy-start(bf16[128,2048]{1,0:T(8,128)(2,1)} %copy-done.3) | copy-start | bytes 1572868
  129.0 28.6 %copy-start.1 = (bf16[384,2048]{1,0:T(8,128)(2,1)S(1)}, bf16[384,2048]{1,0:T(8,128)(2,1)}, u32[]{:S(2)}) copy-start(bf16[384,2048]{1,0:T(8,128)(2,1)} %param.13) | copy-start | bytes 4718596
  129.0 28.7 %copy-start.7 = (f32[2048]{0:T(1024)S(1)}, f32[2048]{0:T(1024)}, u32[]{:S(2)}) copy-start(f32[2048]{0:T(1024)} %param.20) | copy-start | bytes 24580
  132.8 15.8 %collective-permute-start.14 = (bf16[128,2048]{1,0:T(8,128)(2,1)}, bf16[128,2048]{1,0:T(8,128)(2,1)S(1)}, u32[]{:S(2)}, u32[]{:S(2)}) collective-permute-start(bf16[128,2048]{1,0:T(8,128)(2,1)} %collective-permute-done.13), channel_id=1, source_target_pairs={{0,15},{1,0},{2,1},{3,2},{4,3},{5,4},{6,5},{7,6},{8,7},{9,8},{10,9... | collective-permute-start | bytes 1572872 | tf_op jit(solution)/shard_map/ppermute | solution.py:39
  157.7 4.5 copy-start.5
  157.7 4.5 copy-start.6
  167.2 285.3 %reduce-scatter.2.cloned.1.call-start = ((), (), s32[]{:S(2)}) async-start(), calls=%async_computation.2 | async-start | bytes 17825792 | tf_op jit(solution)/shard_map/reduce_scatter | solution.py:82
  167.5 12.9 %copy-start.8 = (s32[384]{0:T(512)S(1)}, s32[384]{0:T(512)}, u32[]{:S(2)}) copy-start(s32[384]{0:T(512)} %param.17) | copy-start | bytes 4612
  184.5 60.0 %all-to-all-start = ((bf16[16,24,2048]{2,1,0:T(8,128)(2,1)}), bf16[16,24,2048]{2,1,0:T(8,128)(2,1)S(1)}, u32[]{:S(2)}, u32[]{:S(2)}) async-start(bf16[16,24,2048]{2,1,0:T(8,128)(2,1)} %bitcast.38), calls=%async_computation | async-start | bytes 3145728 | tf_op jit(solution)/shard_map/all_to_all | solution.py:123
Sparse Core Ops, SparseCore 0:
  167.3 101.5 all-reduce.2
  273.6 178.8 reduce-scatter.1
